TPU v7x, 32 devices: a whole 2x2x4 slice. The times are simulated.
32 devices in a mesh: shard: 8 (over z, y), tensor: 4 (over x, core).
Axes of the slice: x: 2, y: 2, z: 4, core: 2. Of those that a mesh axis runs over, the one named last changes fastest.
Arguments:
- tokens: bfloat16 [12608, 1024], P('shard'), may hold values from -6 to 6
- cotangent: bfloat16 [12608, 1024], P('shard'), may hold values from -6 to 6
- input_weight: float32 [3, 1024, 1024], P(None, 'shard', 'tensor'), may hold values from -2 to 2
- input_moments: float32 [2, 3, 1024, 1024], P(None, None, 'shard', 'tensor'), may hold values from -1 to 1, as said below
- input_bias: float32 [2, 1024], P(None, ('tensor', 'shard')), may hold values from -3 to 3
- input_bias_moments: float32 [2, 2, 1024], P(None, None, ('tensor', 'shard')), may hold values from -1 to 1, as said below
- output_weight: float32 [1024, 1024], P('tensor', 'shard'), may hold values from -0.75 to 0.75
- output_moments: float32 [2, 1024, 1024], P(None, 'tensor', 'shard'), may hold values from -1 to 1, as said below
- expand_weight: float32 [1024, 4096], P('shard', 'tensor'), may hold values from -0.1875 to 0.1875
- expand_moments: float32 [2, 1024, 4096], P(None, 'shard', 'tensor'), may hold values from -1 to 1, as said below
- expand_bias: float32 [4096], P(('tensor', 'shard')), may hold values from -3 to 3
- expand_bias_moments: float32 [2, 4096], P(None, ('tensor', 'shard')), may hold values from -1 to 1, as said below
- shrink_weight: float32 [4096, 1024], P('tensor', 'shard'), may hold values from -0.09375 to 0.09375
- shrink_moments: float32 [2, 4096, 1024], P(None, 'tensor', 'shard'), may hold values from -1 to 1, as said below
- vectors: float32 [6, 1024], P(None, 'shard'), may hold values from -1.2 to 1.4
- vector_moments: float32 [2, 6, 1024], P(None, None, 'shard'), may hold values from -1 to 1, as said below
Outputs:
- block_output: bfloat16 [12608, 1024], P('shard')
- token_gradient: float32 [12608, 1024], P('shard')
- input_weight_gradient: float32 [3, 1024, 1024], P(None, 'shard', 'tensor')
- input_bias_gradient: float32 [2, 1024], P(None, ('tensor', 'shard'))
- output_weight_gradient: float32 [1024, 1024], P('tensor', 'shard')
- expand_weight_gradient: float32 [1024, 4096], P('shard', 'tensor')
- expand_bias_gradient: float32 [4096], P(('tensor', 'shard'))
- shrink_weight_gradient: float32 [4096, 1024], P('tensor', 'shard')
- vectors_gradient: float32 [6, 1024], P(None, 'shard')
- new_input_weight: float32 [3, 1024, 1024], P(None, 'shard', 'tensor')
- new_input_bias: float32 [2, 1024], P(None, ('tensor', 'shard'))
- new_output_weight: float32 [1024, 1024], P('tensor', 'shard')
- new_expand_weight: float32 [1024, 4096], P('shard', 'tensor')
- new_expand_bias: float32 [4096], P(('tensor', 'shard'))
- new_shrink_weight: float32 [4096, 1024], P('tensor', 'shard')
- new_vectors: float32 [6, 1024], P(None, 'shard')
- new_input_moments: float32 [2, 3, 1024, 1024], P(None, None, 'shard', 'tensor')
- new_input_bias_moments: float32 [2, 2, 1024], P(None, None, ('tensor', 'shard'))
- new_output_moments: float32 [2, 1024, 1024], P(None, 'tensor', 'shard')
- new_expand_moments: float32 [2, 1024, 4096], P(None, 'shard', 'tensor')
- new_expand_bias_moments: float32 [2, 4096], P(None, ('tensor', 'shard'))
- new_shrink_moments: float32 [2, 4096, 1024], P(None, 'tensor', 'shard')
- new_vector_moments: float32 [2, 6, 1024], P(None, None, 'shard')
Inputs may be any that keep to these rules, and one draw needn't show every extreme that they name: `input_moments`: second moments positive. `input_bias_moments`: second moments positive. `output_moments`: second moments positive. `expand_moments`: second moments positive. `expand_bias_moments`: second moments positive. `shrink_moments`: second moments positive. `vector_moments`: second moments positive.
All inputs are finite; a program needn't handle non-finite values.
Results may differ from a plain program's by a relative error of at most 0.015.
Values may be sent and summed in bfloat16 or wider, within the bound.
No kernel may reach another device: no remote copies, remote signals or barrier semaphores. Data moves between devices by JAX's collectives and lax.ppermute only.
A program may use at most 192 MiB of HBM per device.

v0:
```python
import jax
import jax.numpy as jnp
from jax import lax
from jax.sharding import PartitionSpec as P

HEAD = 64
SEQ = 197
norm_eps = 1e-06
rate = 0.003
first_decay = 0.9
second_decay = 0.95
weight_decay = 0.05
step_count = 2.0
adam_eps = 1e-08
loss_scale = 128.0


def layer_norm(values, gain, shift):
    row_mean = jnp.mean(values, axis=-1, keepdims=True)
    centred = values - row_mean
    spread = jnp.mean(centred * centred, axis=-1, keepdims=True)
    return centred * lax.rsqrt(spread + norm_eps) * gain + shift


def gelu_exact(values):
    return jax.nn.gelu(values, approximate=False)


def split_heads(values, images):
    return values.reshape(images, SEQ, values.shape[-1] // HEAD, HEAD)


def head_scores(query_heads, key_heads, scale):
    return (
        jnp.einsum("gqhe,gkhe->ghqk", query_heads, key_heads, preferred_element_type=jnp.float32)
        * scale
    )


def adamw(param, moments, grad, decay):
    scaled = grad / loss_scale
    first = first_decay * moments[0] + (1.0 - first_decay) * scaled
    second = second_decay * moments[1] + (1.0 - second_decay) * scaled * scaled
    corrected = (
        first
        / (1.0 - first_decay**step_count)
        / (jnp.sqrt(second / (1.0 - second_decay**step_count)) + adam_eps)
    )
    return (param - rate * (corrected + decay * param), jnp.stack([first, second]))


def on_device(
    tokens,
    cotangent,
    input_weight,
    input_moments,
    input_bias,
    input_bias_moments,
    output_weight,
    output_moments,
    expand_weight,
    expand_moments,
    expand_bias,
    expand_bias_moments,
    shrink_weight,
    shrink_moments,
    vectors,
    vector_moments,
):
    full_input, full_bias, full_output, full_expand, full_expand_bias, full_shrink, full_vectors = (
        lax.all_gather(input_weight.astype(jnp.bfloat16), "shard", axis=1, tiled=True),
        lax.all_gather(input_bias.astype(jnp.bfloat16), "shard", axis=1, tiled=True),
        lax.all_gather(output_weight.astype(jnp.bfloat16), "shard", axis=1, tiled=True),
        lax.all_gather(expand_weight.astype(jnp.bfloat16), "shard", axis=0, tiled=True),
        lax.all_gather(expand_bias.astype(jnp.bfloat16), "shard", axis=0, tiled=True),
        lax.all_gather(shrink_weight.astype(jnp.bfloat16), "shard", axis=1, tiled=True),
        lax.all_gather(vectors.astype(jnp.bfloat16), "shard", axis=1, tiled=True),
    )
    norm_vectors = full_vectors.astype(jnp.float32)
    bias_values = full_bias.astype(jnp.float32)
    rows = tokens.shape[0]
    images = rows // SEQ
    scale = HEAD ** (-0.5)
    start_tokens = tokens.astype(jnp.float32)
    normed, first_back = jax.vjp(layer_norm, start_tokens, norm_vectors[0], norm_vectors[1])
    inputs = normed.astype(jnp.bfloat16)
    project = jnp.einsum("rd,cde->cre", inputs, full_input, preferred_element_type=jnp.float32)
    query = (project[0] + bias_values[0]).astype(jnp.bfloat16)
    keys = project[1].astype(jnp.bfloat16)
    values = (project[2] + bias_values[1]).astype(jnp.bfloat16)
    query_heads = split_heads(query, images)
    key_heads = split_heads(keys, images)
    value_heads = split_heads(values, images)
    scores = head_scores(query_heads, key_heads, scale)
    top = jnp.max(scores, axis=-1, keepdims=True)
    raised = jnp.exp(scores - top)
    total = jnp.sum(raised, axis=-1, keepdims=True)
    attention = (raised / total).astype(jnp.bfloat16)
    log_total = top + jnp.log(total)
    context = jnp.einsum(
        "ghqk,gkhe->gqhe", attention, value_heads, preferred_element_type=jnp.float32
    )
    context = context.reshape(rows, -1).astype(jnp.bfloat16)
    mixed = lax.psum(jnp.dot(context, full_output, preferred_element_type=jnp.float32), "tensor")
    attended = start_tokens + mixed + norm_vectors[2]
    normed_mid, second_back = jax.vjp(layer_norm, attended, norm_vectors[3], norm_vectors[4])
    inputs_mid = normed_mid.astype(jnp.bfloat16)
    pre_act = jnp.dot(
        inputs_mid, full_expand, preferred_element_type=jnp.float32
    ) + full_expand_bias.astype(jnp.float32)
    activated, gelu_back = jax.vjp(gelu_exact, pre_act)
    hidden = activated.astype(jnp.bfloat16)
    shrink_term = jnp.dot(hidden, full_shrink, preferred_element_type=jnp.float32)
    shrunk = lax.psum(shrink_term.astype(jnp.bfloat16), "tensor").astype(jnp.float32)
    block_output = (attended + shrunk + norm_vectors[5]).astype(jnp.bfloat16)
    back_values = cotangent.astype(jnp.float32)
    grad_shrink = jnp.einsum("rf,rd->fd", hidden, cotangent, preferred_element_type=jnp.float32)
    hidden_grad = jnp.einsum(
        "rd,fd->rf", cotangent, full_shrink, preferred_element_type=jnp.float32
    )
    pre_grad = gelu_back(hidden_grad)[0].astype(jnp.bfloat16)
    grad_expand = jnp.einsum("rd,rf->df", inputs_mid, pre_grad, preferred_element_type=jnp.float32)
    grad_expand_bias = jnp.sum(pre_grad.astype(jnp.float32), axis=0)
    mid_part = jnp.einsum("rf,df->rd", pre_grad, full_expand, preferred_element_type=jnp.float32)
    mid_normed_grad = lax.psum(mid_part, "tensor")
    mid_from_norm, gain_two, shift_two = second_back(mid_normed_grad)
    mid_grad = back_values + mid_from_norm
    mid_low = mid_grad.astype(jnp.bfloat16)
    grad_output = jnp.einsum("rk,rd->kd", context, mid_low, preferred_element_type=jnp.float32)
    context_grad = jnp.einsum(
        "rd,kd->rk", mid_low, full_output, preferred_element_type=jnp.float32
    ).astype(jnp.bfloat16)
    context_heads = split_heads(context_grad, images)
    scores = head_scores(query_heads, key_heads, scale)
    probability = jnp.exp(scores - log_total)
    prob_low = probability.astype(jnp.bfloat16)
    prob_grad = jnp.einsum(
        "gqhe,gkhe->ghqk", context_heads, value_heads, preferred_element_type=jnp.float32
    )
    values_grad = jnp.einsum(
        "ghqk,gqhe->gkhe", prob_low, context_heads, preferred_element_type=jnp.float32
    )
    row_dot = jnp.sum(prob_grad * probability, axis=-1, keepdims=True)
    score_grad = (probability * (prob_grad - row_dot)).astype(jnp.bfloat16)
    query_grad = (
        jnp.einsum("ghqk,gkhe->gqhe", score_grad, key_heads, preferred_element_type=jnp.float32)
        * scale
    )
    keys_grad = (
        jnp.einsum("ghqk,gqhe->gkhe", score_grad, query_heads, preferred_element_type=jnp.float32)
        * scale
    )
    project_grad = jnp.stack(
        [query_grad.reshape(rows, -1), keys_grad.reshape(rows, -1), values_grad.reshape(rows, -1)]
    ).astype(jnp.bfloat16)
    grad_bias = jnp.stack(
        [
            jnp.sum(project_grad[0].astype(jnp.float32), axis=0),
            jnp.sum(project_grad[2].astype(jnp.float32), axis=0),
        ]
    )
    grad_input = jnp.einsum("rd,cre->cde", inputs, project_grad, preferred_element_type=jnp.float32)
    input_part = jnp.einsum(
        "cre,cde->rd", project_grad, full_input, preferred_element_type=jnp.float32
    )
    normed_grad = lax.psum(input_part.astype(jnp.bfloat16), "tensor").astype(jnp.float32)
    token_from_norm, gain_one, shift_one = first_back(normed_grad)
    token_gradient = mid_grad + token_from_norm
    grad_vectors = jnp.stack(
        [
            gain_one,
            shift_one,
            jnp.sum(mid_grad, axis=0),
            gain_two,
            shift_two,
            jnp.sum(back_values, axis=0),
        ]
    )
    (
        share_input,
        share_bias,
        share_output,
        share_expand,
        share_expand_bias,
        share_shrink,
        share_vectors,
    ) = (
        lax.psum_scatter(
            grad_input.astype(jnp.bfloat16), "shard", scatter_dimension=1, tiled=True
        ).astype(jnp.float32),
        lax.psum_scatter(
            grad_bias.astype(jnp.bfloat16), "shard", scatter_dimension=1, tiled=True
        ).astype(jnp.float32),
        lax.psum_scatter(
            grad_output.astype(jnp.bfloat16), "shard", scatter_dimension=1, tiled=True
        ).astype(jnp.float32),
        lax.psum_scatter(
            grad_expand.astype(jnp.bfloat16), "shard", scatter_dimension=0, tiled=True
        ).astype(jnp.float32),
        lax.psum_scatter(
            grad_expand_bias.astype(jnp.bfloat16), "shard", scatter_dimension=0, tiled=True
        ).astype(jnp.float32),
        lax.psum_scatter(
            grad_shrink.astype(jnp.bfloat16), "shard", scatter_dimension=1, tiled=True
        ).astype(jnp.float32),
        lax.psum_scatter(
            grad_vectors.astype(jnp.bfloat16), "shard", scatter_dimension=1, tiled=True
        ).astype(jnp.float32),
    )
    new_input, mom_input = adamw(input_weight, input_moments, share_input, weight_decay)
    new_bias, mom_bias = adamw(input_bias, input_bias_moments, share_bias, 0.0)
    new_output, mom_output = adamw(output_weight, output_moments, share_output, weight_decay)
    new_expand, mom_expand = adamw(expand_weight, expand_moments, share_expand, weight_decay)
    new_expand_bias, mom_expand_bias = adamw(
        expand_bias, expand_bias_moments, share_expand_bias, 0.0
    )
    new_shrink, mom_shrink = adamw(shrink_weight, shrink_moments, share_shrink, weight_decay)
    new_vectors, mom_vectors = adamw(vectors, vector_moments, share_vectors, 0.0)
    return (
        block_output,
        token_gradient,
        share_input,
        share_bias,
        share_output,
        share_expand,
        share_expand_bias,
        share_shrink,
        share_vectors,
        new_input,
        new_bias,
        new_output,
        new_expand,
        new_expand_bias,
        new_shrink,
        new_vectors,
        mom_input,
        mom_bias,
        mom_output,
        mom_expand,
        mom_expand_bias,
        mom_shrink,
        mom_vectors,
    )


def solution(mesh):
    return jax.shard_map(
        on_device,
        mesh=mesh,
        in_specs=(
            P("shard", None),
            P("shard", None),
            P(None, "shard", "tensor"),
            P(None, None, "shard", "tensor"),
            P(None, ("tensor", "shard")),
            P(None, None, ("tensor", "shard")),
            P("tensor", "shard"),
            P(None, "tensor", "shard"),
            P("shard", "tensor"),
            P(None, "shard", "tensor"),
            P(("tensor", "shard")),
            P(None, ("tensor", "shard")),
            P("tensor", "shard"),
            P(None, "tensor", "shard"),
            P(None, "shard"),
            P(None, None, "shard"),
        ),
        out_specs=(
            P("shard", None),
            P("shard", None),
            P(None, "shard", "tensor"),
            P(None, ("tensor", "shard")),
            P("tensor", "shard"),
            P("shard", "tensor"),
            P(("tensor", "shard")),
            P("tensor", "shard"),
            P(None, "shard"),
            P(None, "shard", "tensor"),
            P(None, ("tensor", "shard")),
            P("tensor", "shard"),
            P("shard", "tensor"),
            P(("tensor", "shard")),
            P("tensor", "shard"),
            P(None, "shard"),
            P(None, None, "shard", "tensor"),
            P(None, None, ("tensor", "shard")),
            P(None, "tensor", "shard"),
            P(None, "shard", "tensor"),
            P(None, ("tensor", "shard")),
            P(None, "tensor", "shard"),
            P(None, None, "shard"),
        ),
        check_vma=False,
    )
```

profile of v0, /device:TPU:0, one launch (start us, length us, event | category | flops | bytes accessed | tf_op | source)
XLA Modules:
  0.0 1107.1 jit_solution(8191705866244736395)
XLA Ops:
  10.5 22.3 %all-gather = bf16[8,32,2]{1,2,0:T(2,128)(2,1)S(1)} all-gather(bf16[1,32,2]{1,2,0:T(2,128)(2,1)S(1)} %convert_bitcast_fusion.1), channel_id=1, replica_groups=mesh['shard'=8,'tensor'=4] {'shard'}, dimensions={0}, use_global_device_ids=true | all-gather | bytes 1152 | tf_op jit(solution)/shard_map/all_gather | solution.py:72
  34.0 26.5 %all_gather.21 = bf16[6,1024]{1,0:T(8,128)(2,1)S(1)} all-gather(bf16[6,128]{1,0:T(8,128)(2,1)S(1)} %convert_element_type.150), channel_id=1, replica_groups=mesh['shard'=8,'tensor'=4] {'shard'}, dimensions={1}, use_global_device_ids=true | all-gather | bytes 13824 | tf_op jit(solution)/shard_map/all_gather | solution.py:77
  60.5 2.4 convert_reduce_fusion
  64.6 28.1 %all_gather.24 = bf16[256,1024]{1,0:T(8,128)(2,1)} all-gather(bf16[256,128]{1,0:T(8,128)(2,1)S(1)} %convert_element_type.163), channel_id=1, replica_groups=mesh['shard'=8,'tensor'=4] {'shard'}, dimensions={1}, use_global_device_ids=true | all-gather | bytes 589824 | tf_op jit(solution)/shard_map/all_gather | solution.py:73
  92.7 4.9 convolution_bitcast_fusion
  100.5 3.1 copy.127
  103.6 3.7 squeeze.4
  107.3 3.6 reshape.209
  110.9 3.9 copy.132
  114.8 2.7 copy.129
  117.5 3.7 squeeze.5
  132.4 2.9 convert_element_type.162
  135.3 5.1 fusion.85
  144.2 16.4 %all-gather.1 = bf16[8,1,128]{2,1,0:T(2,128)(2,1)S(1)} all-gather(bf16[1,1,128]{2,1,0:T(2,128)(2,1)S(1)} %convert_bitcast_fusion), channel_id=1, replica_groups=mesh['shard'=8,'tensor'=4] {'shard'}, dimensions={0}, use_global_device_ids=true | all-gather | bytes 2304 | tf_op jit(solution)/shard_map/all_gather | solution.py:75
  160.6 100.0 %all-reduce.6.cloned.1.call-done = f32[1576,1024]{1,0:T(8,128)} async-done(((f32[1576,1024]{1,0:T(8,128)}), f32[1576,1024]{1,0:T(8,128)}) %all-reduce.6.cloned.1.call-update) | async-done | bytes 6455312 | tf_op jit(solution)/shard_map/psum | solution.py:104
  260.6 3.8 fusion.77
  267.0 2.5 add_convert_fusion.2
  269.5 43.2 %all-gather.8.cloned.1.call-done = bf16[1024,1024]{1,0:T(8,128)(2,1)} async-done(((bf16[128,1024]{1,0:T(8,128)(2,1)}), bf16[1024,1024]{1,0:T(8,128)(2,1)}) %all-gather.8.cloned.1.call-update) | async-done | bytes 2097168 | tf_op jit(solution)/shard_map/all_gather | solution.py:74
  312.7 8.9 fusion.86
  321.5 42.5 %all-gather.10.cloned.1.call-done = bf16[1024,1024]{1,0:T(8,128)(2,1)} async-done(((bf16[1024,128]{1,0:T(8,128)(2,1)}), bf16[1024,1024]{1,0:T(8,128)(2,1)}) %all-gather.10.cloned.1.call-update) | async-done | bytes 2097168 | tf_op jit(solution)/shard_map/all_gather | solution.py:76
  364.0 21.1 %fusion.74 = (bf16[1024]{0:T(1024)(128)(2,1)S(1)}, bf16[1576,1024]{1,0:T(8,128)(2,1)S(1)}, f32[1576,1024]{1,0:T(8,128)}) fusion(f32[1576,1024]{1,0:T(8,128)} %fusion.86, f32[1024]{0:T(1024)S(1)} %bitcast.225, bf16[1576,1024]{1,0:T(8,128)(2,1)S(1)} %copy-done.7, bf16[1024,1024]{1,0:T(8,128)(2,1)} %all-gather.10.cloned.1.call-done), kind=kOutput, calls=%fused_computation.155 | convolution fusion | flops 3424533504 | bytes 21469184 | tf_op jit(solution)/shard_map/rd,fd->rf/dot_general | solution.py:118
  386.8 5.5 fusion.87
  392.6 9.3 multiply_convert_fusion.1
  401.9 111.0 %all-reduce.8.cloned.1.call-done = f32[1576,1024]{1,0:T(8,128)} async-done(((f32[1576,1024]{1,0:T(8,128)}), f32[1576,1024]{1,0:T(8,128)}) %all-reduce.8.cloned.1.call-update) | async-done | bytes 6455312 | tf_op jit(solution)/shard_map/psum | solution.py:125
  512.9 6.0 multiply_reduce_fusion.1
  519.5 4.6 fusion.76
  524.2 2.7 copy-done.6
  526.9 3.3 convolution_convert_fusion.1
  532.0 2.7 copy.137
  534.8 5.4 fusion.83
  540.2 4.5 multiply_reduce_fusion
  544.9 6.3 multiply_convert_fusion
  554.3 8.3 convolution_convert_fusion.2
  562.6 3.9 copy.174
  566.6 8.3 convolution_convert_fusion.3
  575.1 6.5 fusion.41
  583.7 3.9 copy.167
  587.6 3.7 reshape.197
  591.3 3.4 fusion.40
  594.6 3.9 copy.166
  598.6 3.8 reshape.196
  602.4 3.9 copy.165
  606.3 3.7 reshape.195
  616.4 6.4 fusion.30
  622.8 4.1 copy.168
  626.9 3.2 copy.189
  632.1 2.5 reduce.6
  643.0 21.5 %all-reduce = bf16[1024]{0:T(1024)(128)(2,1)S(1)} all-reduce(bf16[1024]{0:T(1024)(128)(2,1)S(1)} %get-tuple-element.138), channel_id=6, replica_groups=mesh['shard'=8,'tensor'=4] {'shard'}, use_global_device_ids=true, to_apply=%region_22.0.clone | all-reduce | flops 1024 | bytes 4096
  664.5 8.0 convolution_convert_fusion
  672.5 4.2 bitcast_convert_fusion
  681.7 6.1 reduce-scatter.25.cloned.1.call-done
  689.0 70.1 %reduce-scatter.17.cloned.1.call-done = bf16[128,1024]{1,0:T(8,128)(2,1)} async-done(((bf16[1024,1024]{1,0:T(8,128)(2,1)}), bf16[128,1024]{1,0:T(8,128)(2,1)}) %reduce-scatter.17.cloned.1.call-update) | async-done | bytes 262160 | tf_op jit(solution)/shard_map/reduce_scatter | solution.py:197
  760.5 2.8 fusion.56
  766.7 58.0 %reduce-scatter.23.cloned.1.call-done = bf16[128,256]{1,0:T(8,128)(2,1)} async-done(((bf16[1024,256]{1,0:T(8,128)(2,1)}), bf16[128,256]{1,0:T(8,128)(2,1)}) %reduce-scatter.23.cloned.1.call-update) | async-done | bytes 65552
  829.2 63.3 %reduce-scatter.19.cloned.1.call-done = bf16[128,768]{1,0:T(8,128)(2,1)} async-done(((bf16[1024,768]{1,0:T(8,128)(2,1)}), bf16[128,768]{1,0:T(8,128)(2,1)}) %reduce-scatter.19.cloned.1.call-update) | async-done | bytes 196624
  896.2 2.3 fusion.52
  899.5 2.5 copy.159
  903.9 112.7 %all-reduce.10.cloned.1.call-done = (bf16[1576,1024]{1,0:T(8,128)(2,1)}, bf16[1576,1024]{1,0:T(8,128)(2,1)}) async-done(((bf16[1576,1024]{1,0:T(8,128)(2,1)}, bf16[1576,1024]{1,0:T(8,128)(2,1)}), (bf16[1576,1024]{1,0:T(8,128)(2,1)}, bf16[1576,1024]{1,0:T(8,128)(2,1)})) %all-reduce.10.cloned.1.call-update) | async-done | bytes 6455312 | tf_op jit(solution)/shard_map/psum | solution.py:114
  1016.6 2.5 reduce.5
  1019.1 3.5 fusion.10
  1022.7 3.4 fusion.8
  1026.2 8.3 fusion.73
  1035.5 6.7 add_convert_fusion.1
  1042.2 55.7 %reduce-scatter.27.cloned.1.call-done = bf16[128,6]{1,0:T(8,128)(2,1)} async-done(((bf16[1024,6]{1,0:T(8,128)(2,1)}), bf16[128,6]{1,0:T(8,128)(2,1)}) %reduce-scatter.27.cloned.1.call-update) | async-done | bytes 1552
  (226 shorter events, 77.5 us)
Async XLA Ops:
  7.2 55.8 %copy-start.2 = (bf16[1576,1024]{1,0:T(8,128)(2,1)S(1)}, bf16[1576,1024]{1,0:T(8,128)(2,1)}, u32[]{:S(2)}) copy-start(bf16[1576,1024]{1,0:T(8,128)(2,1)} %param.16) | copy-start | bytes 9682948
  7.2 85.5 %all-gather.6.cloned.1.call-start = ((), (), s32[]{:S(2)}) async-start(), calls=%async_computation.6 | async-start | bytes 1769472 | tf_op jit(solution)/shard_map/all_gather | solution.py:71
  9.1 251.5 %all-reduce.6.cloned.1.call-start = ((), (), s32[]{:S(2)}) async-start(), calls=%async_computation.7 | async-start | bytes 12910592 | tf_op jit(solution)/shard_map/psum | solution.py:104
  63.0 34.6 %copy-start.21 = (f32[1576]{0:T(1024)}, f32[1576]{0:T(1024)S(1)}, u32[]{:S(2)}) copy-start(f32[1576]{0:T(1024)S(1)} %broadcast_multiply_fusion.1) | copy-start | bytes 18916
  64.0 33.6 %copy-start.24 = (f32[1576]{0:T(1024)}, f32[1576]{0:T(1024)S(1)}, u32[]{:S(2)}) copy-start(f32[1576]{0:T(1024)S(1)} %fusion.60) | copy-start | bytes 18916
  64.6 33.0 %copy-start.29 = (f32[1,1024]{1,0:T(1,128)}, f32[1,1024]{1,0:T(1,128)S(1)}, u32[]{:S(2)}) copy-start(f32[1,1024]{1,0:T(1,128)S(1)} %get-tuple-element.164) | copy-start | bytes 12292
  64.6 33.0 %copy-start.44 = (f32[1,1024]{1,0:T(1,128)}, f32[1,1024]{1,0:T(1,128)S(1)}, u32[]{:S(2)}) copy-start(f32[1,1024]{1,0:T(1,128)S(1)} %get-tuple-element.165) | copy-start | bytes 12292
  121.2 5.4 copy-start.10
  123.2 6.0 copy-start.12
  127.8 3.0 copy-start.1
  140.4 3.8 copy-start.50
  140.4 172.2 %all-gather.8.cloned.1.call-start = ((), (), s32[]{:S(2)}) async-start(), calls=%async_computation.8 | async-start | bytes 2359296 | tf_op jit(solution)/shard_map/all_gather | solution.py:74
  142.3 221.8 %all-gather.10.cloned.1.call-start = ((), (), s32[]{:S(2)}) async-start(), calls=%async_computation.9 | async-start | bytes 2359296 | tf_op jit(solution)/shard_map/all_gather | solution.py:76
  144.1 368.8 %all-reduce.8.cloned.1.call-start = ((), (), s32[]{:S(2)}) async-start(), calls=%async_computation.10 | async-start | bytes 12910592 | tf_op jit(solution)/shard_map/psum | solution.py:125
  264.4 2.6 copy-start
  269.5 94.6 %copy-start.7 = (bf16[1576,1024]{1,0:T(8,128)(2,1)S(1)}, bf16[1576,1024]{1,0:T(8,128)(2,1)}, u32[]{:S(2)}) copy-start(bf16[1576,1024]{1,0:T(8,128)(2,1)} %param.17) | copy-start | bytes 9682948
  364.0 22.8 %copy-start.52 = (bf16[1024,1024]{1,0:T(8,128)(2,1)S(1)}, bf16[1024,1024]{1,0:T(8,128)(2,1)}, u32[]{:S(2)}) copy-start(bf16[1024,1024]{1,0:T(8,128)(2,1)} %all-gather.8.cloned.1.call-done) | copy-start | bytes 6291460
  385.1 1.6 copy-start.55
  392.3 287.4 %reduce-scatter.21.cloned.1.call-start = ((), (), s32[]{:S(2)}) async-start(), calls=%async_computation.13 | async-start | bytes 73728
  512.9 6.6 copy-start.5
  519.5 7.4 copy-start.15
  524.1 2.8 copy-start.6
  524.1 51.0 %copy-start.32 = (f32[1576]{0:T(1024)}, f32[1576]{0:T(1024)S(1)}, u32[]{:S(2)}) copy-start(f32[1576]{0:T(1024)S(1)} %negate_multiply_fusion.2) | copy-start | bytes 18916
  530.2 10.1 slice-start
  534.8 5.4 copy-start.13
  534.8 5.4 slice-start.1
  544.9 6.4 copy-start.11
  553.8 134.0 %reduce-scatter.25.cloned.1.call-start = ((), (), s32[]{:S(2)}) async-start(), calls=%async_computation.15 | async-start | bytes 2359296
  566.5 192.6 %reduce-scatter.17.cloned.1.call-start = ((), (), s32[]{:S(2)}) async-start(), calls=%async_computation.11 | async-start | bytes 2359296 | tf_op jit(solution)/shard_map/reduce_scatter | solution.py:197
  574.9 249.8 %reduce-scatter.23.cloned.1.call-start = ((), (), s32[]{:S(2)}) async-start(), calls=%async_computation.14 | async-start | bytes 589824
  598.5 17.8 %copy-start.3 = (bf16[1576,1024]{1,0:T(8,128)(2,1)S(1)}, bf16[1576,1024]{1,0:T(8,128)(2,1)}, u32[]{:S(2)}) copy-start(bf16[1576,1024]{1,0:T(8,128)(2,1)} %param.16) | copy-start | bytes 9682948
  598.5 17.8 %copy-start.22 = (f32[1576]{0:T(1024)S(1)}, f32[1576]{0:T(1024)}, u32[]{:S(2)}) copy-start(f32[1576]{0:T(1024)} %copy-done.21) | copy-start | bytes 18916
  598.5 17.8 %copy-start.25 = (f32[1576]{0:T(1024)S(1)}, f32[1576]{0:T(1024)}, u32[]{:S(2)}) copy-start(f32[1576]{0:T(1024)} %copy-done.24) | copy-start | bytes 18916
  598.5 17.8 %copy-start.30 = (f32[1,1024]{1,0:T(1,128)S(1)}, f32[1,1024]{1,0:T(1,128)}, u32[]{:S(2)}) copy-start(f32[1,1024]{1,0:T(1,128)} %copy-done.29) | copy-start | bytes 12292
  598.6 17.8 %copy-start.45 = (f32[1,1024]{1,0:T(1,128)S(1)}, f32[1,1024]{1,0:T(1,128)}, u32[]{:S(2)}) copy-start(f32[1,1024]{1,0:T(1,128)} %copy-done.44) | copy-start | bytes 12292
  612.1 280.4 %reduce-scatter.19.cloned.1.call-start = ((), (), s32[]{:S(2)}) async-start(), calls=%async_computation.12 | async-start | bytes 1769472
  626.9 14.2 %copy-start.54 = (u32[32]{0:T(128)S(1)}, u32[32]{0:T(128)}, u32[]{:S(2)}) copy-start(u32[32]{0:T(128)} %constant.97) | copy-start | bytes 388
  626.9 15.5 %copy-start.42 = (f32[2,6,128]{2,0,1:T(2,128)S(1)}, f32[2,6,128]{2,0,1:T(2,128)}, u32[]{:S(2)}) copy-start(f32[2,6,128]{2,0,1:T(2,128)} %param.31) | copy-start | bytes 18436
  626.9 37.6 %copy-start.47 = (f32[2,128]{1,0:T(2,128)S(1)}, f32[2,128]{1,0:T(2,128)}, u32[]{:S(2)}) copy-start(f32[2,128]{1,0:T(2,128)} %param.27) | copy-start | bytes 3076
  630.1 386.5 %all-reduce.10.cloned.1.call-start = ((), (), s32[]{:S(2)}) async-start(), calls=%async_computation.17 | async-start | bytes 12910592 | tf_op jit(solution)/shard_map/psum | solution.py:114
  664.5 12.5 %copy-start.48 = (f32[128]{0:T(128)}, f32[128]{0:T(128)S(1)}, u32[]{:S(2)}) copy-start(f32[128]{0:T(128)S(1)} %get-tuple-element.129) | copy-start | bytes 1540
  664.5 8.0 copy-start.20
  664.5 8.0 copy-start.53
  676.8 3.7 copy-start.43
  676.8 3.8 copy-start.49
  676.8 421.1 %reduce-scatter.27.cloned.1.call-start = ((), (), s32[]{:S(2)}) async-start(), calls=%async_computation.16 | async-start | bytes 294912
  759.1 5.2 copy-start.14
  759.1 5.3 copy-start.18
  760.5 5.2 copy-start.16
  826.6 196.1 %copy-start.19 = (f32[256,128]{1,0:T(8,128)}, f32[256,128]{1,0:T(8,128)S(1)}, u32[]{:S(2)}) copy-start(f32[256,128]{1,0:T(8,128)S(1)} %get-tuple-element.133) | copy-start | bytes 393220
  898.5 120.6 %copy-start.23 = (f32[1576]{0:T(1024)S(1)}, f32[1576]{0:T(1024)}, u32[]{:S(2)}) copy-start(f32[1576]{0:T(1024)} %copy-done.21) | copy-start | bytes 18916
  898.5 120.6 %copy-start.31 = (f32[1,1024]{1,0:T(1,128)S(1)}, f32[1,1024]{1,0:T(1,128)}, u32[]{:S(2)}) copy-start(f32[1,1024]{1,0:T(1,128)} %copy-done.29) | copy-start | bytes 12292
  898.5 124.1 %copy-start.28 = (f32[1576]{0:T(1024)S(1)}, f32[1576]{0:T(1024)}, u32[]{:S(2)}) copy-start(f32[1576]{0:T(1024)} %copy-done.27) | copy-start | bytes 18916
  898.5 124.2 %copy-start.26 = (f32[1576]{0:T(1024)S(1)}, f32[1576]{0:T(1024)}, u32[]{:S(2)}) copy-start(f32[1576]{0:T(1024)} %copy-done.24) | copy-start | bytes 18916
  1019.1 3.6 copy-start.4
  1019.1 7.1 copy-start.8
  1019.1 7.1 copy-start.33
  1026.2 8.3 copy-start.36
  1026.2 8.3 copy-start.37
  1026.2 8.3 copy-start.38
  1026.2 9.3 copy-start.35
  1035.5 63.3 %copy-start.34 = (f32[1,6,128]{2,0,1:T(1,128)S(1)}, f32[1,6,128]{2,0,1:T(1,128)}, u32[]{:S(2)}) copy-start(f32[1,6,128]{2,0,1:T(1,128)} %get-tuple-element.169) | copy-start | bytes 9220
  1035.5 63.3 %copy-start.39 = (f32[6,128]{1,0:T(8,128)S(1)}, f32[6,128]{1,0:T(8,128)}, u32[]{:S(2)}) copy-start(f32[6,128]{1,0:T(8,128)} %param.30) | copy-start | bytes 9220
  1035.5 63.3 %copy-start.41 = (f32[1,6,128]{2,0,1:T(1,128)S(1)}, f32[1,6,128]{2,0,1:T(1,128)}, u32[]{:S(2)}) copy-start(f32[1,6,128]{2,0,1:T(1,128)} %get-tuple-element.168) | copy-start | bytes 9220
  (6 other events, 5.5 us)
Sparse Core Ops, SparseCore 0:
  10.8 46.9 all-gather.5
  140.5 120.0 all-reduce.5
  263.3 49.2 all-gather.7
  315.1 48.8 all-gather.9
  392.4 120.4 all-reduce.7
  554.0 62.6 reduce-scatter.20
  620.2 67.5 reduce-scatter.24
  691.4 67.6 reduce-scatter.16
  763.0 61.6 reduce-scatter.22
  828.0 64.4 reduce-scatter.18
  895.5 121.0 all-reduce.9
  1035.6 62.2 reduce-scatter.26
where the time goes:
time: 1110 us
  waiting for transfers between devices  663 us (60%)
  blocking collectives  115 us (10%)
  local copies, waits for them, and re-layouts  109 us (10%)
  matrix products  108 us (10%)
  other arithmetic  94.5 us (9%)
  between operations  15.8 us (1%)
    unnamed x17, waiting for transfers between devices  183 us
    psum x1, waiting for transfers between devices, on_device(): lax.psum(shrink_term.astype(jnp.bfloat16), 'tensor').astype(jnp.float32)  113 us
    psum x1, waiting for transfers between devices, on_device(): mid_normed_grad = lax.psum(mid_part, 'tensor')  111 us
    psum x1, waiting for transfers between devices, on_device(): lax.psum(jnp.dot(context, full_output, preferred_element_type=jnp.float32...  100 us
    reduce_scatter x1, waiting for transfers between devices, on_device(): lax.psum_scatter(grad_expand.astype(jnp.bfloat16), 'shard', scatter_dimen...  70.1 us
    unnamed x138, local copies, waits for them, and re-layouts  46.1 us
    all_gather x1, waiting for transfers between devices, on_device(): lax.all_gather(expand_weight.astype(jnp.bfloat16), 'shard', axis=0, tiled...  43.2 us
    all_gather x1, waiting for transfers between devices, on_device(): lax.all_gather(shrink_weight.astype(jnp.bfloat16), 'shard', axis=1, tiled...  42.5 us
  transfers between devices with their start and end apart: 12, of which 10 were waited for; matrix products, arithmetic and copies ran while one was open for 15% of the time, Pallas kernels for 0%

commit v1 on v0

--- a/solution.py
+++ b/solution.py
@@ -122,7 +122,11 @@
     grad_expand = jnp.einsum("rd,rf->df", inputs_mid, pre_grad, preferred_element_type=jnp.float32)
     grad_expand_bias = jnp.sum(pre_grad.astype(jnp.float32), axis=0)
     mid_part = jnp.einsum("rf,df->rd", pre_grad, full_expand, preferred_element_type=jnp.float32)
-    mid_normed_grad = lax.psum(mid_part, "tensor")
+    mid_normed_grad = mid_part
+    n = lax.axis_size("tensor")
+    for q in [[(k, k ^ p) for k in range(n)] for p in (1, 2, 4, 8, 16) if p < n]:
+        carry_out = lax.ppermute(mid_normed_grad, "tensor", q)
+        mid_normed_grad = mid_normed_grad + carry_out
     mid_from_norm, gain_two, shift_two = second_back(mid_normed_grad)
     mid_grad = back_values + mid_from_norm
     mid_low = mid_grad.astype(jnp.bfloat16)

time: 1110 us -> 1020 us (0.919)
  waiting for transfers between devices: 663 us -> 573 us
    ppermute x0 -> x2, waiting for transfers between devices: none -> 124 us  [on_device(): carry_out = lax.ppermute(mid_normed_grad, 'tensor', q)]
    psum x1 -> x0, waiting for transfers between devices: 111 us -> none  [on_device(): mid_normed_grad = lax.psum(mid_part, 'tensor')]
    reduce_scatter x1, waiting for transfers between devices: 70.1 us -> 0.02 us  [on_device(): lax.psum_scatter(grad_expand.astype(jnp.bfloat16), 'shard', scatter_dimen...]
    unnamed x17 -> x16, waiting for transfers between devices: 183 us -> 151 us
    unnamed x138 -> x140, local copies, waits for them, and re-layouts: 46.1 us -> 48.9 us
  transfers between devices with their start and end apart: 12 -> 13, of which waited for: 10 -> 9; matrix products, arithmetic and copies ran while one was open for 15% -> 20% of each run, Pallas kernels for 0% -> 0%
where the time goes in v1:
time: 1020 us
  waiting for transfers between devices  573 us (56%)
  blocking collectives  112 us (11%)
  local copies, waits for them, and re-layouts  109 us (11%)
  matrix products  107 us (10%)
  other arithmetic  96.1 us (9%)
  between operations  15.6 us (2%)
    unnamed x16, waiting for transfers between devices  151 us
    ppermute x2, waiting for transfers between devices, on_device(): carry_out = lax.ppermute(mid_normed_grad, 'tensor', q)  124 us
    psum x1, waiting for transfers between devices, on_device(): lax.psum(shrink_term.astype(jnp.bfloat16), 'tensor').astype(jnp.float32)  113 us
    psum x1, waiting for transfers between devices, on_device(): lax.psum(jnp.dot(context, full_output, preferred_element_type=jnp.float32...  99.9 us
    unnamed x140, local copies, waits for them, and re-layouts  48.9 us
    all_gather x1, waiting for transfers between devices, on_device(): lax.all_gather(expand_weight.astype(jnp.bfloat16), 'shard', axis=0, tiled...  43.2 us
    all_gather x1, waiting for transfers between devices, on_device(): lax.all_gather(shrink_weight.astype(jnp.bfloat16), 'shard', axis=1, tiled...  42.5 us
    all_gather x1, blocking collectives, on_device(): lax.all_gather(output_weight.astype(jnp.bfloat16), 'shard', axis=1, tiled...  28.1 us
  transfers between devices with their start and end apart: 13, of which 9 were waited for; matrix products, arithmetic and copies ran while one was open for 20% of the time, Pallas kernels for 0%

profile of v1, /device:TPU:0, one launch (start us, length us, event | category | flops | bytes accessed | tf_op | source)
XLA Modules:
  0.0 1016.0 jit_solution(18152789051629115109)
XLA Ops:
  10.5 22.3 %all-gather = bf16[8,32,2]{1,2,0:T(2,128)(2,1)S(1)} all-gather(bf16[1,32,2]{1,2,0:T(2,128)(2,1)S(1)} %convert_bitcast_fusion.1), channel_id=1, replica_groups=mesh['shard'=8,'tensor'=4] {'shard'}, dimensions={0}, use_global_device_ids=true | all-gather | bytes 1152 | tf_op jit(solution)/shard_map/all_gather | solution.py:72
  34.0 26.5 %all_gather.21 = bf16[6,1024]{1,0:T(8,128)(2,1)S(1)} all-gather(bf16[6,128]{1,0:T(8,128)(2,1)S(1)} %convert_element_type.150), channel_id=1, replica_groups=mesh['shard'=8,'tensor'=4] {'shard'}, dimensions={1}, use_global_device_ids=true | all-gather | bytes 13824 | tf_op jit(solution)/shard_map/all_gather | solution.py:77
  60.5 2.4 convert_reduce_fusion
  64.6 28.1 %all_gather.24 = bf16[256,1024]{1,0:T(8,128)(2,1)} all-gather(bf16[256,128]{1,0:T(8,128)(2,1)S(1)} %convert_element_type.163), channel_id=1, replica_groups=mesh['shard'=8,'tensor'=4] {'shard'}, dimensions={1}, use_global_device_ids=true | all-gather | bytes 589824 | tf_op jit(solution)/shard_map/all_gather | solution.py:73
  92.7 4.9 convolution_bitcast_fusion
  100.5 2.8 copy.127
  103.3 3.7 squeeze.4
  107.0 3.6 reshape.209
  110.6 3.9 copy.132
  114.5 2.7 copy.129
  117.2 3.7 squeeze.5
  122.9 2.3 add_convert_fusion.3
  132.0 2.9 convert_element_type.162
  134.9 5.1 fusion.85
  143.8 16.5 %all-gather.1 = bf16[8,1,128]{2,1,0:T(2,128)(2,1)S(1)} all-gather(bf16[1,1,128]{2,1,0:T(2,128)(2,1)S(1)} %convert_bitcast_fusion), channel_id=1, replica_groups=mesh['shard'=8,'tensor'=4] {'shard'}, dimensions={0}, use_global_device_ids=true | all-gather | bytes 2304 | tf_op jit(solution)/shard_map/all_gather | solution.py:75
  160.3 99.9 %all-reduce.5.cloned.1.call-done = f32[1576,1024]{1,0:T(8,128)} async-done(((f32[1576,1024]{1,0:T(8,128)}), f32[1576,1024]{1,0:T(8,128)}) %all-reduce.5.cloned.1.call-update) | async-done | bytes 6455312 | tf_op jit(solution)/shard_map/psum | solution.py:104
  260.2 3.8 fusion.77
  266.6 2.5 add_convert_fusion.2
  269.1 43.2 %all-gather.8.cloned.1.call-done = bf16[1024,1024]{1,0:T(8,128)(2,1)} async-done(((bf16[128,1024]{1,0:T(8,128)(2,1)}), bf16[1024,1024]{1,0:T(8,128)(2,1)}) %all-gather.8.cloned.1.call-update) | async-done | bytes 2097168 | tf_op jit(solution)/shard_map/all_gather | solution.py:74
  312.3 8.9 fusion.86
  321.1 42.5 %all-gather.10.cloned.1.call-done = bf16[1024,1024]{1,0:T(8,128)(2,1)} async-done(((bf16[1024,128]{1,0:T(8,128)(2,1)}), bf16[1024,1024]{1,0:T(8,128)(2,1)}) %all-gather.10.cloned.1.call-update) | async-done | bytes 2097168 | tf_op jit(solution)/shard_map/all_gather | solution.py:76
  363.7 21.5 %fusion.74 = (bf16[1024]{0:T(1024)(128)(2,1)S(1)}, bf16[1576,1024]{1,0:T(8,128)(2,1)S(1)}, f32[1576,1024]{1,0:T(8,128)}) fusion(f32[1576,1024]{1,0:T(8,128)} %fusion.86, f32[1024]{0:T(1024)S(1)} %bitcast.225, bf16[1576,1024]{1,0:T(8,128)(2,1)S(1)} %copy-done.7, bf16[1024,1024]{1,0:T(8,128)(2,1)} %all-gather.10.cloned.1.call-done), kind=kOutput, calls=%fused_computation.155 | convolution fusion | flops 3424533504 | bytes 21469184 | tf_op jit(solution)/shard_map/rd,fd->rf/dot_general | solution.py:118
  386.8 3.6 fusion.87
  390.6 10.4 %collective-permute-done = f32[1576,1024]{1,0:T(8,128)S(1)} collective-permute-done((f32[1576,1024]{1,0:T(8,128)S(1)}, f32[1576,1024]{1,0:T(8,128)S(1)}, u32[]{:S(2)}, u32[]{:S(2)}) %collective-permute-start) | collective-permute-done | bytes 6455328 | tf_op jit(solution)/shard_map/ppermute | solution.py:128
  400.9 4.2 add.265
  406.7 6.4 multiply_convert_fusion.1
  414.8 5.3 convolution_convert_fusion.2
  420.1 4.0 copy.174
  424.2 8.2 convolution_convert_fusion.3
  432.7 113.9 %collective-permute-done.1 = f32[1576,1024]{1,0:T(8,128)} collective-permute-done((f32[1576,1024]{1,0:T(8,128)}, f32[1576,1024]{1,0:T(8,128)}, u32[]{:S(2)}, u32[]{:S(2)}) %collective-permute-start.1) | collective-permute-done | bytes 6455328 | tf_op jit(solution)/shard_map/ppermute | solution.py:128
  546.6 7.9 multiply_reduce_fusion.1
  554.5 4.7 fusion.76
  559.3 2.7 copy-done.6
  562.0 3.3 convolution_convert_fusion.1
  567.0 5.4 fusion.83
  572.5 7.9 multiply_reduce_fusion
  580.4 4.6 multiply_convert_fusion
  589.3 4.1 copy.165
  593.4 4.0 reshape.195
  597.4 4.4 fusion.40
  601.8 5.6 fusion.41
  611.6 4.1 copy.167
  615.7 3.7 reshape.197
  619.3 3.9 copy.166
  623.2 3.7 reshape.196
  631.2 6.4 fusion.30
  637.7 4.1 copy.168
  641.8 3.2 copy.189
  646.9 2.5 reduce.6
  657.8 18.7 %all-reduce = bf16[1024]{0:T(1024)(128)(2,1)S(1)} all-reduce(bf16[1024]{0:T(1024)(128)(2,1)S(1)} %get-tuple-element.138), channel_id=6, replica_groups=mesh['shard'=8,'tensor'=4] {'shard'}, use_global_device_ids=true, to_apply=%region_21.0.clone | all-reduce | flops 1024 | bytes 4096
  676.6 8.0 convolution_convert_fusion
  684.6 4.2 bitcast_convert_fusion
  693.1 2.8 fusion.56
  702.5 31.4 %reduce-scatter.23.cloned.1.call-done = bf16[128,256]{1,0:T(8,128)(2,1)} async-done(((bf16[1024,256]{1,0:T(8,128)(2,1)}), bf16[128,256]{1,0:T(8,128)(2,1)}) %reduce-scatter.23.cloned.1.call-update) | async-done | bytes 65552
  738.4 63.4 %reduce-scatter.19.cloned.1.call-done = bf16[128,768]{1,0:T(8,128)(2,1)} async-done(((bf16[1024,768]{1,0:T(8,128)(2,1)}), bf16[128,768]{1,0:T(8,128)(2,1)}) %reduce-scatter.19.cloned.1.call-update) | async-done | bytes 196624
  805.6 2.3 fusion.52
  808.9 2.5 copy.159
  813.3 112.5 %all-reduce.7.cloned.1.call-done = (bf16[1576,1024]{1,0:T(8,128)(2,1)}, bf16[1576,1024]{1,0:T(8,128)(2,1)}) async-done(((bf16[1576,1024]{1,0:T(8,128)(2,1)}, bf16[1576,1024]{1,0:T(8,128)(2,1)}), (bf16[1576,1024]{1,0:T(8,128)(2,1)}, bf16[1576,1024]{1,0:T(8,128)(2,1)})) %all-reduce.7.cloned.1.call-update) | async-done | bytes 6455312 | tf_op jit(solution)/shard_map/psum | solution.py:114
  925.8 2.5 reduce.5
  928.3 3.5 fusion.10
  931.9 3.4 fusion.8
  935.4 8.3 fusion.73
  944.8 6.7 add_convert_fusion.1
  951.4 55.7 %reduce-scatter.27.cloned.1.call-done = bf16[128,6]{1,0:T(8,128)(2,1)} async-done(((bf16[1024,6]{1,0:T(8,128)(2,1)}), bf16[128,6]{1,0:T(8,128)(2,1)}) %reduce-scatter.27.cloned.1.call-update) | async-done | bytes 1552
  (230 shorter events, 78.7 us)
Async XLA Ops:
  7.2 55.8 %copy-start.2 = (bf16[1576,1024]{1,0:T(8,128)(2,1)S(1)}, bf16[1576,1024]{1,0:T(8,128)(2,1)}, u32[]{:S(2)}) copy-start(bf16[1576,1024]{1,0:T(8,128)(2,1)} %param.16) | copy-start | bytes 9682948
  7.2 85.5 %all-gather.6.cloned.1.call-start = ((), (), s32[]{:S(2)}) async-start(), calls=%async_computation.6 | async-start | bytes 1769472 | tf_op jit(solution)/shard_map/all_gather | solution.py:71
  9.1 251.1 %all-reduce.5.cloned.1.call-start = ((), (), s32[]{:S(2)}) async-start(), calls=%async_computation.7 | async-start | bytes 12910592 | tf_op jit(solution)/shard_map/psum | solution.py:104
  63.0 34.6 %copy-start.22 = (f32[1576]{0:T(1024)}, f32[1576]{0:T(1024)S(1)}, u32[]{:S(2)}) copy-start(f32[1576]{0:T(1024)S(1)} %broadcast_multiply_fusion.1) | copy-start | bytes 18916
  64.0 33.6 %copy-start.25 = (f32[1576]{0:T(1024)}, f32[1576]{0:T(1024)S(1)}, u32[]{:S(2)}) copy-start(f32[1576]{0:T(1024)S(1)} %fusion.60) | copy-start | bytes 18916
  64.6 33.0 %copy-start.30 = (f32[1,1024]{1,0:T(1,128)}, f32[1,1024]{1,0:T(1,128)S(1)}, u32[]{:S(2)}) copy-start(f32[1,1024]{1,0:T(1,128)S(1)} %get-tuple-element.165) | copy-start | bytes 12292
  64.6 33.0 %copy-start.45 = (f32[1,1024]{1,0:T(1,128)}, f32[1,1024]{1,0:T(1,128)S(1)}, u32[]{:S(2)}) copy-start(f32[1,1024]{1,0:T(1,128)S(1)} %get-tuple-element.166) | copy-start | bytes 12292
  120.9 5.3 copy-start.11
  122.9 5.9 copy-start.13
  127.5 3.0 copy-start.1
  140.0 3.8 copy-start.51
  140.0 172.2 %all-gather.8.cloned.1.call-start = ((), (), s32[]{:S(2)}) async-start(), calls=%async_computation.8 | async-start | bytes 2359296 | tf_op jit(solution)/shard_map/all_gather | solution.py:74
  141.9 221.8 %all-gather.10.cloned.1.call-start = ((), (), s32[]{:S(2)}) async-start(), calls=%async_computation.9 | async-start | bytes 2359296 | tf_op jit(solution)/shard_map/all_gather | solution.py:76
  143.7 546.8 %reduce-scatter.25.cloned.1.call-start = ((), (), s32[]{:S(2)}) async-start(), calls=%async_computation.14 | async-start | bytes 2359296
  264.0 2.6 copy-start
  269.1 94.6 %copy-start.7 = (bf16[1576,1024]{1,0:T(8,128)(2,1)S(1)}, bf16[1576,1024]{1,0:T(8,128)(2,1)}, u32[]{:S(2)}) copy-start(bf16[1576,1024]{1,0:T(8,128)(2,1)} %param.17) | copy-start | bytes 9682948
  363.7 23.2 %copy-start.53 = (bf16[1024,1024]{1,0:T(8,128)(2,1)S(1)}, bf16[1024,1024]{1,0:T(8,128)(2,1)}, u32[]{:S(2)}) copy-start(bf16[1024,1024]{1,0:T(8,128)(2,1)} %all-gather.8.cloned.1.call-done) | copy-start | bytes 6291460
  390.5 10.5 %collective-permute-start = (f32[1576,1024]{1,0:T(8,128)S(1)}, f32[1576,1024]{1,0:T(8,128)S(1)}, u32[]{:S(2)}, u32[]{:S(2)}) collective-permute-start(f32[1576,1024]{1,0:T(8,128)S(1)} %fusion.87), channel_id=1, source_target_pairs={{0,1},{1,0},{2,3},{3,2},{4,5},{5,4},{6,7},{7,6},{8,9},{9,8},{10,11... | collective-permute-start | bytes 19365896 | tf_op jit(solution)/shard_map/ppermute | solution.py:128
  405.2 141.4 %collective-permute-start.1 = (f32[1576,1024]{1,0:T(8,128)}, f32[1576,1024]{1,0:T(8,128)}, u32[]{:S(2)}, u32[]{:S(2)}) collective-permute-start(f32[1576,1024]{1,0:T(8,128)} %add.265), channel_id=1, source_target_pairs={{0,2},{1,3},{2,0},{3,1},{4,6},{5,7},{6,4},{7,5},{8,10},{9,11},{10,... | collective-permute-start | bytes 19365896 | tf_op jit(solution)/shard_map/ppermute | solution.py:128
  424.1 267.6 %reduce-scatter.17.cloned.1.call-start = ((), (), s32[]{:S(2)}) async-start(), calls=%async_computation.10 | async-start | bytes 2359296 | tf_op jit(solution)/shard_map/reduce_scatter | solution.py:201
  432.4 268.1 %reduce-scatter.21.cloned.1.call-start = ((), (), s32[]{:S(2)}) async-start(), calls=%async_computation.12 | async-start | bytes 73728
  554.5 7.5 copy-start.16
  559.2 2.8 copy-start.6
  559.3 42.5 %copy-start.33 = (f32[1576]{0:T(1024)}, f32[1576]{0:T(1024)S(1)}, u32[]{:S(2)}) copy-start(f32[1576]{0:T(1024)S(1)} %negate_multiply_fusion.2) | copy-start | bytes 18916
  567.0 13.4 %slice-start = ((s8[6553600]{0:T(1024)(128)(4,1)}), s8[2359296]{0:T(1024)(128)(4,1)S(1)}, s32[]{:S(2)}) async-start(s8[6553600]{0:T(1024)(128)(4,1)} %bitcast.197), calls=%async_computation.17 | async-start | bytes 4718592
  572.5 7.9 slice-start.1
  580.4 6.3 copy-start.12
  588.5 13.3 %copy-start.8 = (bf16[1576,1024]{1,0:T(8,128)(2,1)S(1)}, bf16[1576,1024]{1,0:T(8,128)(2,1)}, u32[]{:S(2)}) copy-start(bf16[1576,1024]{1,0:T(8,128)(2,1)} %param.17) | copy-start | bytes 9682948
  607.4 126.5 %reduce-scatter.23.cloned.1.call-start = ((), (), s32[]{:S(2)}) async-start(), calls=%async_computation.13 | async-start | bytes 589824
  611.6 19.6 %copy-start.3 = (bf16[1576,1024]{1,0:T(8,128)(2,1)S(1)}, bf16[1576,1024]{1,0:T(8,128)(2,1)}, u32[]{:S(2)}) copy-start(bf16[1576,1024]{1,0:T(8,128)(2,1)} %param.16) | copy-start | bytes 9682948
  611.6 19.6 %copy-start.23 = (f32[1576]{0:T(1024)S(1)}, f32[1576]{0:T(1024)}, u32[]{:S(2)}) copy-start(f32[1576]{0:T(1024)} %copy-done.22) | copy-start | bytes 18916
  611.6 19.6 %copy-start.26 = (f32[1576]{0:T(1024)S(1)}, f32[1576]{0:T(1024)}, u32[]{:S(2)}) copy-start(f32[1576]{0:T(1024)} %copy-done.25) | copy-start | bytes 18916
  611.6 19.6 %copy-start.31 = (f32[1,1024]{1,0:T(1,128)S(1)}, f32[1,1024]{1,0:T(1,128)}, u32[]{:S(2)}) copy-start(f32[1,1024]{1,0:T(1,128)} %copy-done.30) | copy-start | bytes 12292
  611.6 19.6 %copy-start.46 = (f32[1,1024]{1,0:T(1,128)S(1)}, f32[1,1024]{1,0:T(1,128)}, u32[]{:S(2)}) copy-start(f32[1,1024]{1,0:T(1,128)} %copy-done.45) | copy-start | bytes 12292
  626.9 174.9 %reduce-scatter.19.cloned.1.call-start = ((), (), s32[]{:S(2)}) async-start(), calls=%async_computation.11 | async-start | bytes 1769472
  641.8 14.2 %copy-start.55 = (u32[32]{0:T(128)S(1)}, u32[32]{0:T(128)}, u32[]{:S(2)}) copy-start(u32[32]{0:T(128)} %constant.97) | copy-start | bytes 388
  641.8 15.4 %copy-start.43 = (f32[2,6,128]{2,0,1:T(2,128)S(1)}, f32[2,6,128]{2,0,1:T(2,128)}, u32[]{:S(2)}) copy-start(f32[2,6,128]{2,0,1:T(2,128)} %param.31) | copy-start | bytes 18436
  641.8 34.7 %copy-start.48 = (f32[2,128]{1,0:T(2,128)S(1)}, f32[2,128]{1,0:T(2,128)}, u32[]{:S(2)}) copy-start(f32[2,128]{1,0:T(2,128)} %param.27) | copy-start | bytes 3076
  645.0 280.8 %all-reduce.7.cloned.1.call-start = ((), (), s32[]{:S(2)}) async-start(), calls=%async_computation.16 | async-start | bytes 12910592 | tf_op jit(solution)/shard_map/psum | solution.py:114
  676.6 12.5 %copy-start.49 = (f32[128]{0:T(128)}, f32[128]{0:T(128)S(1)}, u32[]{:S(2)}) copy-start(f32[128]{0:T(128)S(1)} %get-tuple-element.129) | copy-start | bytes 1540
  676.6 8.0 copy-start.21
  676.6 8.0 copy-start.54
  688.8 318.3 %reduce-scatter.27.cloned.1.call-start = ((), (), s32[]{:S(2)}) async-start(), calls=%async_computation.15 | async-start | bytes 294912
  691.7 5.2 copy-start.15
  691.7 5.3 copy-start.19
  693.1 5.2 copy-start.17
  693.1 8.2 copy-start.44
  693.1 8.2 copy-start.50
  701.3 32.6 %copy-start.47 = (f32[2,32]{1,0:T(2,128)}, f32[2,32]{1,0:T(2,128)S(1)}, u32[]{:S(2)}) copy-start(f32[2,32]{1,0:T(2,128)S(1)} %get-tuple-element.135) | copy-start | bytes 772
  735.8 196.1 %copy-start.20 = (f32[256,128]{1,0:T(8,128)}, f32[256,128]{1,0:T(8,128)S(1)}, u32[]{:S(2)}) copy-start(f32[256,128]{1,0:T(8,128)S(1)} %get-tuple-element.133) | copy-start | bytes 393220
  807.9 120.4 %copy-start.24 = (f32[1576]{0:T(1024)S(1)}, f32[1576]{0:T(1024)}, u32[]{:S(2)}) copy-start(f32[1576]{0:T(1024)} %copy-done.22) | copy-start | bytes 18916
  807.9 120.4 %copy-start.32 = (f32[1,1024]{1,0:T(1,128)S(1)}, f32[1,1024]{1,0:T(1,128)}, u32[]{:S(2)}) copy-start(f32[1,1024]{1,0:T(1,128)} %copy-done.30) | copy-start | bytes 12292
  807.9 124.0 %copy-start.29 = (f32[1576]{0:T(1024)S(1)}, f32[1576]{0:T(1024)}, u32[]{:S(2)}) copy-start(f32[1576]{0:T(1024)} %copy-done.28) | copy-start | bytes 18916
  807.9 124.0 %copy-start.27 = (f32[1576]{0:T(1024)S(1)}, f32[1576]{0:T(1024)}, u32[]{:S(2)}) copy-start(f32[1576]{0:T(1024)} %copy-done.25) | copy-start | bytes 18916
  928.3 3.6 copy-start.4
  928.3 7.1 copy-start.9
  928.3 7.1 copy-start.34
  935.4 8.3 copy-start.37
  935.4 8.3 copy-start.38
  935.4 8.3 copy-start.39
  935.4 9.3 copy-start.36
  944.7 63.3 %copy-start.35 = (f32[1,6,128]{2,0,1:T(1,128)S(1)}, f32[1,6,128]{2,0,1:T(1,128)}, u32[]{:S(2)}) copy-start(f32[1,6,128]{2,0,1:T(1,128)} %get-tuple-element.170) | copy-start | bytes 9220
  944.7 63.3 %copy-start.40 = (f32[6,128]{1,0:T(8,128)S(1)}, f32[6,128]{1,0:T(8,128)}, u32[]{:S(2)}) copy-start(f32[6,128]{1,0:T(8,128)} %param.30) | copy-start | bytes 9220
  944.7 63.3 %copy-start.42 = (f32[1,6,128]{2,0,1:T(1,128)S(1)}, f32[1,6,128]{2,0,1:T(1,128)}, u32[]{:S(2)}) copy-start(f32[1,6,128]{2,0,1:T(1,128)} %get-tuple-element.169) | copy-start | bytes 9220
  (8 other events, 9.8 us)
Sparse Core Ops, SparseCore 0:
  10.8 46.9 all-gather.5
  140.2 120.0 all-reduce.4
  262.9 49.2 all-gather.7
  314.8 48.8 all-gather.9
  424.2 65.5 reduce-scatter.24
  493.2 67.4 reduce-scatter.16
  607.5 60.7 reduce-scatter.20
  672.2 61.6 reduce-scatter.22
  737.3 64.4 reduce-scatter.18
  804.7 121.0 all-reduce.6
  944.8 62.2 reduce-scatter.26
